TPU v7x, 256 devices: a whole 4x4x8 slice. The times are simulated.
256 devices in a mesh: dp: 16 (over y, x_lo, core), feat: 16 (over x_hi, z).
Axes of the slice: x: 4 (x_hi: 2, x_lo: 2; x = x_hi * 2 + x_lo), y: 4, z: 8, core: 2. Of those that a mesh axis runs over, the one named last changes fastest.
Arguments:
- tokens: bfloat16 [8192, 16384], P('dp', 'feat'), may hold values from -6 to 6
- weight: bfloat16 [32, 6, 512, 512], P('feat'), may hold values from -0.15625 to 0.15625
- cotangent: bfloat16 [8192, 16384], P('dp', 'feat'), may hold values from -6 to 6
Outputs:
- output: bfloat16 [8192, 16384], P('dp', 'feat')
- input_grad: bfloat16 [8192, 16384], P('dp', 'feat')
- weight_grad: float32 [32, 6, 512, 512], P('feat', None, 'dp')
All inputs are finite; a program needn't handle non-finite values.
Results may differ from a plain program's by a relative error of at most 0.0057.
Values may be sent and summed in bfloat16 or wider, within the bound.
A program may use at most 128 MiB of HBM per device.

v0:
```python
from functools import partial

import jax
import jax.numpy as jnp
import numpy as np
from jax import lax
from jax.sharding import PartitionSpec as P

PARTNERS = 6


gelu_tanh = partial(jax.nn.gelu, approximate=True)


def swapped(value, axis, apart):
    mask = 2**apart
    pairs = [(source, source ^ mask) for source in range(lax.axis_size(axis))]
    return lax.ppermute(value, axis, pairs)


def neighbours(blocks):
    per_device = blocks.shape[1]
    result = [blocks]
    for bit_pos in range(PARTNERS - 1):
        distance = 1 << bit_pos
        if distance < per_device:
            result.append(blocks[:, np.arange(per_device) ^ distance, :])
        else:
            level = (distance // per_device).bit_length() - 1
            result.append(swapped(blocks, "feat", level))
    return result


def mix_layer(parts, weight):
    total = jnp.einsum("tnb,nbc->tnc", parts[0], weight[:, 0], preferred_element_type=jnp.float32)
    for which in range(1, PARTNERS):
        total = total + jnp.einsum(
            "tnb,nbc->tnc", parts[which], weight[:, which], preferred_element_type=jnp.float32
        )
    return total


def back_sum(delta, weight):
    per_device = delta.shape[1]
    total = (
        jnp.einsum("tnc,nbc->tnb", delta, weight[:, 0], preferred_element_type=jnp.float32)
        .astype(jnp.bfloat16)
        .astype(jnp.float32)
    )
    for bit_pos in range(PARTNERS - 1):
        distance = 1 << bit_pos
        term = jnp.einsum(
            "tnc,nbc->tnb", delta, weight[:, bit_pos + 1], preferred_element_type=jnp.float32
        ).astype(jnp.bfloat16)
        if distance < per_device:
            arrived = term[:, np.arange(per_device) ^ distance, :]
        else:
            level = (distance // per_device).bit_length() - 1
            arrived = swapped(term, "feat", level)
        total = total + arrived.astype(jnp.float32)
    return total


def local(tokens, weight, cotangent):
    tok_rows = tokens.shape[0]
    per_device = weight.shape[0]
    block_width = weight.shape[2]
    inputs = tokens.reshape(tok_rows, per_device, block_width)
    parts = neighbours(inputs)
    z_value = mix_layer(parts, weight)
    output = gelu_tanh(z_value).astype(jnp.bfloat16)
    unused, pull_back = jax.vjp(gelu_tanh, z_value)
    delta = pull_back(cotangent.reshape(tok_rows, per_device, block_width).astype(jnp.float32))[
        0
    ].astype(jnp.bfloat16)
    local_all = jnp.stack(
        [
            jnp.einsum("tnb,tnc->nbc", parts[which], delta, preferred_element_type=jnp.float32)
            for which in range(PARTNERS)
        ],
        axis=1,
    )
    weight_grad = lax.psum_scatter(local_all, "dp", scatter_dimension=2, tiled=True)
    input_grad = back_sum(delta, weight).astype(jnp.bfloat16)
    return (
        output.reshape(tok_rows, per_device * block_width),
        input_grad.reshape(tok_rows, per_device * block_width),
        weight_grad,
    )


def solution(mesh):
    return jax.shard_map(
        local,
        mesh=mesh,
        in_specs=(P("dp", "feat"), P("feat", None, None, None), P("dp", "feat")),
        out_specs=(P("dp", "feat"), P("dp", "feat"), P("feat", None, "dp", None)),
        check_vma=False,
    )
```

profile of v0, /device:TPU:32, one launch (start us, length us, event | category | flops | bytes accessed | tf_op | source)
XLA Modules:
  0.0 469.2 jit_solution(1972624248445403433)
XLA Ops:
  7.2 0.0 all-reduce.3.cloned.1.call-start
  7.2 1.5 copy.77
  8.7 1.3 copy.82
  10.0 0.0 copy-start.7
  10.0 6.3 %collective-permute-start.2 = (bf16[512,2,512]{2,0,1:T(8,128)(2,1)}, bf16[512,2,512]{2,0,1:T(8,128)(2,1)}, u32[]{:S(2)}, u32[]{:S(2)}) collective-permute-start(bf16[512,2,512]{2,0,1:T(8,128)(2,1)} %copy.82), channel_id=1, source_target_pairs={{0,4},{1,5},{2,6},{3,7},{4,0},{5,1},{6,2},{7,3},{8,12},{9,13},{10,... | collective-permute-start | bytes 3145736 | tf_op jit(solution)/shard_map/ppermute | solution.py:18
  16.3 1.5 collective-permute-start.1
  17.8 1.0 collective-permute-start
  18.8 3.0 collective-permute-start.3
  21.8 3.3 fusion.31
  25.1 0.0 copy-done.7
  25.2 0.6 gather_fusion
  25.8 3.3 fusion.28
  29.1 2.6 copy.89
  31.7 32.0 %collective-permute-done.2 = bf16[512,2,512]{2,0,1:T(8,128)(2,1)} collective-permute-done((bf16[512,2,512]{2,0,1:T(8,128)(2,1)}, bf16[512,2,512]{2,0,1:T(8,128)(2,1)}, u32[]{:S(2)}, u32[]{:S(2)}) %collective-permute-start.2) | collective-permute-done | bytes 1048608 | tf_op jit(solution)/shard_map/ppermute | solution.py:18
  63.7 2.4 fusion.19
  66.2 40.2 %collective-permute-done.1 = bf16[512,2,512]{2,0,1:T(8,128)(2,1)} collective-permute-done((bf16[512,2,512]{2,0,1:T(8,128)(2,1)}, bf16[512,2,512]{2,0,1:T(8,128)(2,1)}, u32[]{:S(2)}, u32[]{:S(2)}) %collective-permute-start.1) | collective-permute-done | bytes 1048608 | tf_op jit(solution)/shard_map/ppermute | solution.py:18
  106.4 0.0 copy-start.2
  106.4 2.6 fusion.22
  109.0 0.0 copy-start
  109.0 0.0 copy-start.1
  109.0 0.0 collective-permute-done
  109.0 2.6 fusion.25
  111.6 0.0 collective-permute-done.3
  111.6 0.0 copy-start.4
  111.7 1.0 copy-done.4
  112.6 0.0 copy-done.2
  112.6 0.0 copy-done
  112.6 0.0 copy-done.1
  112.6 4.9 %fusion.6 = (bf16[512,2,512]{0,2,1:T(8,128)(2,1)S(1)}, bf16[512,2,512]{0,2,1:T(8,128)(2,1)}) fusion(f32[512,2,512]{0,2,1:T(8,128)S(1)} %bitcast.142, bf16[512,2,512]{2,0,1:T(8,128)(2,1)} %copy-done.4, bf16[2,6,512,512]{3,2,1,0:T(8,128)(2,1)} %param.8, f32[2,512,512]{2,1,0:T(8,128)S(1)} %fusion.19, f32[2,512,512]{2,1,0:T(8,128)S(1)} %fusion.22, ...), kind=kOutput, calls=%fused_computation.10 | convolution fusion | flops 551026688 | bytes 16777216 | tf_op jit(solution)/shard_map/tnb,nbc->tnc/dot_general | solution.py:37
  117.6 2.1 bitcast_dynamic-update-slice_fusion.4
  119.6 2.0 bitcast_dynamic-update-slice_fusion.5
  121.7 3.3 bitcast_dynamic-update-slice_fusion.3
  125.0 3.3 bitcast_dynamic-update-slice_fusion.2
  128.2 0.0 copy-start.5
  128.2 3.4 bitcast_dynamic-update-slice_fusion.1
  131.6 0.0 copy-done.5
  131.6 2.1 bitcast_dynamic-update-slice_fusion
  133.7 19.2 %copy.110 = f32[2,6,512,512]{3,0,1,2:T(2,128)} copy(f32[2,6,512,512]{2,3,0,1:T(8,128)} %bitcast_dynamic-update-slice_fusion) | data formatting | bytes 25165824 | tf_op jit(solution)/shard_map/stack | solution.py:76
  152.9 0.0 all-reduce.3.cloned.1.call-update
  152.9 2.9 fusion.12
  155.8 3.0 fusion.13
  158.8 2.9 fusion.14
  161.7 3.0 fusion.15
  164.7 2.8 collective-permute-start.4
  167.5 0.6 collective-permute-start.5
  168.1 1.4 collective-permute-start.6
  169.5 3.0 collective-permute-start.7
  172.5 0.0 copy-done.8
  172.5 0.6 dynamic-slice
  173.8 3.1 fusion.11
  176.9 1.9 gather_fusion.1
  178.8 1.3 copy.94
  180.1 0.0 copy-done.3
  180.1 1.3 copy.111
  181.4 31.8 %collective-permute-done.4 = bf16[512,2,512]{0,2,1:T(8,128)(2,1)} collective-permute-done((bf16[512,2,512]{0,2,1:T(8,128)(2,1)}, bf16[512,2,512]{0,2,1:T(8,128)(2,1)}, u32[]{:S(2)}, u32[]{:S(2)}) %collective-permute-start.4) | collective-permute-done | bytes 1048608 | tf_op jit(solution)/shard_map/ppermute | solution.py:18
  213.2 45.3 %collective-permute-done.5 = bf16[512,2,512]{0,2,1:T(8,128)(2,1)} collective-permute-done((bf16[512,2,512]{0,2,1:T(8,128)(2,1)}, bf16[512,2,512]{0,2,1:T(8,128)(2,1)}, u32[]{:S(2)}, u32[]{:S(2)}) %collective-permute-start.5) | collective-permute-done | bytes 1048608 | tf_op jit(solution)/shard_map/ppermute | solution.py:18
  258.5 1.3 collective-permute-done.6
  259.8 0.0 collective-permute-done.7
  259.9 0.0 copy-done.6
  259.9 3.7 fusion.10
  263.5 1.3 copy.112
  264.8 195.0 %all-reduce.3.cloned.1.call-done = f32[2,6,512,512]{3,0,1,2:T(2,128)} async-done(((f32[2,6,512,512]{3,0,1,2:T(2,128)}), f32[2,6,512,512]{3,0,1,2:T(2,128)}) %all-reduce.3.cloned.1.call-update) | async-done | bytes 12582928
  459.8 1.4 constant_dynamic-slice_fusion
  461.2 1.1 copy.113
  (4 shorter events, 0.0 us)
Async XLA Ops:
  7.2 452.7 %all-reduce.3.cloned.1.call-start = ((), (), s32[]{:S(2)}) async-start(), calls=%async_computation | async-start | bytes 25165824
  10.0 15.1 %copy-start.7 = (s32[2]{0:T(128)S(1)}, s32[2]{0:T(128)}, u32[]{:S(2)}) copy-start(s32[2]{0:T(128)} %constant.22) | copy-start | bytes 28
  10.0 53.7 %collective-permute-start.2 = (bf16[512,2,512]{2,0,1:T(8,128)(2,1)}, bf16[512,2,512]{2,0,1:T(8,128)(2,1)}, u32[]{:S(2)}, u32[]{:S(2)}) collective-permute-start(bf16[512,2,512]{2,0,1:T(8,128)(2,1)} %copy.82), channel_id=1, source_target_pairs={{0,4},{1,5},{2,6},{3,7},{4,0},{5,1},{6,2},{7,3},{8,12},{9,13},{10,... | collective-permute-start | bytes 3145736 | tf_op jit(solution)/shard_map/ppermute | solution.py:18
  16.3 90.1 %collective-permute-start.1 = (bf16[512,2,512]{2,0,1:T(8,128)(2,1)}, bf16[512,2,512]{2,0,1:T(8,128)(2,1)}, u32[]{:S(2)}, u32[]{:S(2)}) collective-permute-start(bf16[512,2,512]{2,0,1:T(8,128)(2,1)} %copy.82), channel_id=1, source_target_pairs={{0,2},{1,3},{2,0},{3,1},{4,6},{5,7},{6,4},{7,5},{8,10},{9,11},{10,... | collective-permute-start | bytes 3145736 | tf_op jit(solution)/shard_map/ppermute | solution.py:18
  17.8 91.2 %collective-permute-start = (bf16[512,2,512]{2,0,1:T(8,128)(2,1)}, bf16[512,2,512]{2,0,1:T(8,128)(2,1)}, u32[]{:S(2)}, u32[]{:S(2)}) collective-permute-start(bf16[512,2,512]{2,0,1:T(8,128)(2,1)} %copy.82), channel_id=1, source_target_pairs={{0,1},{1,0},{2,3},{3,2},{4,5},{5,4},{6,7},{7,6},{8,9},{9,8},{10,11... | collective-permute-start | bytes 3145736 | tf_op jit(solution)/shard_map/ppermute | solution.py:18
  18.8 92.8 %collective-permute-start.3 = (bf16[512,2,512]{2,0,1:T(8,128)(2,1)}, bf16[512,2,512]{2,0,1:T(8,128)(2,1)S(1)}, u32[]{:S(2)}, u32[]{:S(2)}) collective-permute-start(bf16[512,2,512]{2,0,1:T(8,128)(2,1)} %copy.82), channel_id=1, source_target_pairs={{0,8},{1,9},{2,10},{3,11},{4,12},{5,13},{6,14},{7,15},{8,0},{9,1},... | collective-permute-start | bytes 3145736 | tf_op jit(solution)/shard_map/ppermute | solution.py:18
  106.4 6.2 %copy-start.2 = (f32[512,1024]{0,1:T(8,128)S(1)}, f32[512,1024]{0,1:T(8,128)}, u32[]{:S(2)}) copy-start(f32[512,1024]{0,1:T(8,128)} %copy.89) | copy-start | bytes 6291460
  109.0 3.6 copy-start
  109.0 3.6 copy-start.1
  111.6 1.0 copy-start.4
  128.2 3.4 copy-start.5
  161.7 10.8 %copy-start.8 = (u32[256]{0:T(256)S(1)}, u32[256]{0:T(256)}, u32[]{:S(2)}) copy-start(u32[256]{0:T(256)} %constant.26) | copy-start | bytes 3076
  164.7 48.5 %collective-permute-start.4 = (bf16[512,2,512]{0,2,1:T(8,128)(2,1)}, bf16[512,2,512]{0,2,1:T(8,128)(2,1)}, u32[]{:S(2)}, u32[]{:S(2)}) collective-permute-start(bf16[512,2,512]{0,2,1:T(8,128)(2,1)} %fusion.12), channel_id=1, source_target_pairs={{0,1},{1,0},{2,3},{3,2},{4,5},{5,4},{6,7},{7,6},{8,9},{9,8},{10,11... | collective-permute-start | bytes 3145736 | tf_op jit(solution)/shard_map/ppermute | solution.py:18
  167.5 91.0 %collective-permute-start.5 = (bf16[512,2,512]{0,2,1:T(8,128)(2,1)}, bf16[512,2,512]{0,2,1:T(8,128)(2,1)}, u32[]{:S(2)}, u32[]{:S(2)}) collective-permute-start(bf16[512,2,512]{0,2,1:T(8,128)(2,1)} %fusion.13), channel_id=1, source_target_pairs={{0,2},{1,3},{2,0},{3,1},{4,6},{5,7},{6,4},{7,5},{8,10},{9,11},{10,... | collective-permute-start | bytes 3145736 | tf_op jit(solution)/shard_map/ppermute | solution.py:18
  168.1 91.7 %collective-permute-start.6 = (bf16[512,2,512]{0,2,1:T(8,128)(2,1)}, bf16[512,2,512]{0,2,1:T(8,128)(2,1)}, u32[]{:S(2)}, u32[]{:S(2)}) collective-permute-start(bf16[512,2,512]{0,2,1:T(8,128)(2,1)} %fusion.14), channel_id=1, source_target_pairs={{0,4},{1,5},{2,6},{3,7},{4,0},{5,1},{6,2},{7,3},{8,12},{9,13},{10,... | collective-permute-start | bytes 3145736 | tf_op jit(solution)/shard_map/ppermute | solution.py:18
  169.5 90.3 %collective-permute-start.7 = (bf16[512,2,512]{0,2,1:T(8,128)(2,1)}, bf16[512,2,512]{0,2,1:T(8,128)(2,1)}, u32[]{:S(2)}, u32[]{:S(2)}) collective-permute-start(bf16[512,2,512]{0,2,1:T(8,128)(2,1)} %fusion.15), channel_id=1, source_target_pairs={{0,8},{1,9},{2,10},{3,11},{4,12},{5,13},{6,14},{7,15},{8,0},{9,1},... | collective-permute-start | bytes 3145736 | tf_op jit(solution)/shard_map/ppermute | solution.py:18
  176.9 3.3 copy-start.3
  180.1 79.7 %copy-start.6 = (bf16[2,512,512]{1,2,0:T(8,128)(2,1)S(1)}, bf16[2,512,512]{1,2,0:T(8,128)(2,1)}, u32[]{:S(2)}) copy-start(bf16[2,512,512]{1,2,0:T(8,128)(2,1)} %copy.94) | copy-start | bytes 3145732
Sparse Core Ops, SparseCore 0:
  153.0 306.7 all-reduce.2
where the time goes:
time: 470 us; the launch traced here: 469 us
  waiting for transfers between devices  346 us (74%)
  matrix products  53.8 us (11%)
  local copies, waits for them, and re-layouts  35.2 us (7%)
  starting transfers between devices  19.6 us (4%)
  between operations  14.8 us (3%)
    unnamed x2, waiting for transfers between devices  195 us
    ppermute x8, waiting for transfers between devices, swapped(): return lax.ppermute(value, axis, pairs)  151 us
    ppermute x8, starting transfers between devices, swapped(): return lax.ppermute(value, axis, pairs)  19.6 us
    another operation x1, local copies, waits for them, and re-layouts, local(): jnp.stack([jnp.einsum('tnb,tnc->nbc', parts[which], delta, preferred_elem...  19.2 us
    dot_general x6, matrix products, local(): jnp.einsum('tnb,tnc->nbc', parts[which], delta, preferred_element_type=jn...  16.1 us
    dot_general x5, matrix products, mix_layer(): jnp.einsum('tnb,nbc->tnc', parts[which], weight[:, which], preferred_elem...  15.9 us
    dot_general x5, matrix products, back_sum(): jnp.einsum('tnc,nbc->tnb', delta, weight[:, bit_pos + 1], preferred_eleme...  14.9 us
  transfers between devices with their start and end apart: 9, of which 6 were waited for; matrix products, arithmetic and copies ran while one was open for 9% of the time, Pallas kernels for 0%

commit v1 on v0

v1 whole, which is shorter than its diff:
```python
import functools

import jax
import jax.numpy as jnp
from jax import lax
from jax.experimental import pallas as pl
from jax.experimental.pallas import tpu as pltpu
from jax.sharding import PartitionSpec as P

F32 = jnp.float32
BF16 = jnp.bfloat16
MESH = pl.DeviceIdType.MESH
BLK = 512
PARTNERS = 6
CHUNKS = 8
REMOTE = 4
CHIPS = 8
SLOPE = 0.7978845608028654
CUBE = 0.044715


def flip(value, bit):
    return value + bit - 2 * bit * ((value // bit) % 2)


def nn(a, b):
    return lax.dot_general(a, b, (((1,), (0,)), ((), ())), preferred_element_type=F32)


def nt(a, b):
    return lax.dot_general(a, b, (((1,), (1,)), ((), ())), preferred_element_type=F32)


def tn(a, b):
    return lax.dot_general(a, b, (((0,), (0,)), ((), ())), preferred_element_type=F32)


def kernel(
    tok_hbm, w_hbm, cot_hbm, out_hbm, ig_hbm, wg_hbm,
    tok, w, cot, trecv, delta, outv, acc, tsend, termrecv, mine, other, crecv, total, rsrecv, wgv,
    load_sem, store_sem, tok_ssem, tok_rsem, term_ssem, term_rsem, c_ssem, c_rsem, rs_ssem, rs_rsem,
):
    rows = tok.shape[0] // CHUNKS
    d = lax.axis_index("dp")
    f = lax.axis_index("feat")
    core = d % 2
    chip = d // 2
    y = chip // 2
    x_lo = chip % 2

    partners = [(d, flip(f, 1 << b)) for b in range(REMOTE)]
    core_mate = (flip(d, 1), f)

    def chip_of(j):
        dy, dx = j // 2, j % 2
        return ((y + dy) % 4) * 2 + (x_lo + dx) % 2

    def mate(j):
        return (chip_of(j) * 2 + core, f)

    everyone = partners + [core_mate]
    barrier = pltpu.get_barrier_semaphore()
    for who in everyone:
        pl.semaphore_signal(barrier, inc=1, device_id=who, device_id_type=MESH)
    for j in range(1, CHIPS):
        pl.semaphore_signal(barrier, inc=1, device_id=mate(j), device_id_type=MESH)

    load_tok = pltpu.make_async_copy(tok_hbm, tok, load_sem.at[0])
    load_w = pltpu.make_async_copy(w_hbm, w, load_sem.at[1])
    load_cot = pltpu.make_async_copy(cot_hbm, cot, load_sem.at[2])
    load_tok.start()
    load_w.start()
    load_cot.start()
    pl.semaphore_wait(barrier, len(everyone) + CHIPS - 1)
    load_tok.wait()

    def span(c):
        return pl.ds(pl.multiple_of(c * rows, rows), rows)

    def tok_copy(b, c):
        return pltpu.make_async_remote_copy(
            src_ref=tok.at[span(c)], dst_ref=trecv.at[b, span(c)],
            send_sem=tok_ssem.at[b, c], recv_sem=tok_rsem.at[b, c],
            device_id=partners[b], device_id_type=MESH,
        )

    def term_copy(b, c):
        return pltpu.make_async_remote_copy(
            src_ref=tsend.at[b, span(c)], dst_ref=termrecv.at[b, span(c)],
            send_sem=term_ssem.at[b, c], recv_sem=term_rsem.at[b, c],
            device_id=partners[b], device_id_type=MESH,
        )

    @pl.loop(0, CHUNKS)
    def _(c):
        for b in (2, 1, 0, 3):
            tok_copy(b, c).start()

    load_w.wait()
    load_cot.wait()

    def half(n):
        return pl.ds(n * BLK, BLK)

    @pl.loop(0, CHUNKS)
    def _(c):
        here = span(c)
        for b in range(REMOTE):
            tok_copy(b, c).wait_recv()
        for n in range(2):
            z = nn(tok[here, half(n)], w[n, 0]) + nn(tok[here, half(1 - n)], w[n, 1])
            for b in range(REMOTE):
                z = z + nn(trecv[b, here, half(n)], w[n, b + 2])
            square = z * z
            t = jnp.tanh(SLOPE * (z + CUBE * (square * z)))
            outv[here, half(n)] = (0.5 * z * (1.0 + t)).astype(BF16)
            slope = 0.5 * (1.0 + t) + 0.5 * z * (1.0 - t * t) * (SLOPE * (1.0 + 3.0 * CUBE * square))
            delta[here, half(n)] = (cot[here, half(n)].astype(F32) * slope).astype(BF16)
        for b in (2, 1, 0, 3):
            for n in range(2):
                tsend[b, here, half(n)] = nt(delta[here, half(n)], w[n, b + 2]).astype(BF16)
            term_copy(b, c).start()
        for n in range(2):
            own = nt(delta[here, half(n)], w[n, 0]).astype(BF16).astype(F32)
            side = nt(delta[here, half(1 - n)], w[1 - n, 1]).astype(BF16).astype(F32)
            acc[here, half(n)] = own + side

    store_out = pltpu.make_async_copy(outv, out_hbm, store_sem.at[0])
    store_out.start()

    def core_copy(k):
        return pltpu.make_async_remote_copy(
            src_ref=other.at[k], dst_ref=crecv.at[k],
            send_sem=c_ssem.at[k], recv_sem=c_rsem.at[k],
            device_id=core_mate, device_id_type=MESH,
        )

    def rs_copy(k, j):
        return pltpu.make_async_remote_copy(
            src_ref=total.at[k, chip_of(j)], dst_ref=rsrecv.at[j - 1, k],
            send_sem=rs_ssem.at[j - 1, k], recv_sem=rs_rsem.at[j - 1, k],
            device_id=mate(j), device_id_type=MESH,
        )

    for k in range(PARTNERS):
        for n in range(2):
            if k == 0:
                left = tok[:, half(n)]
            elif k == 1:
                left = tok[:, half(1 - n)]
            else:
                left = trecv[k - 2, :, half(n)]
            grad = tn(left, delta[:, half(n)])
            grad = grad.reshape(CHIPS, 2, BLK // 16, BLK)
            even, odd = grad[:, 0], grad[:, 1]
            mine[k, :, n] = jnp.where(core == 0, even, odd)
            other[k, :, n] = jnp.where(core == 0, odd, even).astype(BF16)
        core_copy(k).start()

    @pl.loop(0, PARTNERS)
    def _(k):
        core_copy(k).wait_recv()
        for q in range(CHIPS):
            both = mine[k, q] + crecv[k, q].astype(F32)
            mine[k, q] = both
            total[k, q] = both.astype(BF16)
        for j in range(1, CHIPS):
            rs_copy(k, j).start()

    @pl.loop(0, CHUNKS)
    def _(c):
        here = span(c)
        for b in range(REMOTE):
            term_copy(b, c).wait_recv()
        result = acc[here, :]
        for b in range(REMOTE):
            result = result + termrecv[b, here].astype(F32)
        cot[here, :] = result.astype(BF16)

    store_ig = pltpu.make_async_copy(cot, ig_hbm, store_sem.at[1])
    store_ig.start()

    @pl.loop(0, PARTNERS)
    def _(k):
        for j in range(1, CHIPS):
            rs_copy(k, j).wait_recv()
        summed = mine[k, chip]
        for j in range(1, CHIPS):
            summed = summed + rsrecv[j - 1, k].astype(F32)
        for n in range(2):
            wgv[n, k] = summed[n]

    store_wg = pltpu.make_async_copy(wgv, wg_hbm, store_sem.at[2])
    store_wg.start()

    @pl.loop(0, CHUNKS)
    def _(c):
        for b in range(REMOTE):
            tok_copy(b, c).wait_send()
            term_copy(b, c).wait_send()

    @pl.loop(0, PARTNERS)
    def _(k):
        core_copy(k).wait_send()
        for j in range(1, CHIPS):
            rs_copy(k, j).wait_send()

    store_out.wait()
    store_ig.wait()
    store_wg.wait()


def local(tokens, weight, cotangent):
    r, width = tokens.shape
    strip = BLK // 16
    dma = pltpu.SemaphoreType.DMA
    return pl.pallas_call(
        kernel,
        out_shape=(
            jax.ShapeDtypeStruct((r, width), BF16),
            jax.ShapeDtypeStruct((r, width), BF16),
            jax.ShapeDtypeStruct((2, PARTNERS, strip, BLK), F32),
        ),
        in_specs=[pl.BlockSpec(memory_space=pl.ANY)] * 3,
        out_specs=[pl.BlockSpec(memory_space=pl.ANY)] * 3,
        scratch_shapes=[
            pltpu.VMEM((r, width), BF16),
            pltpu.VMEM(weight.shape, BF16),
            pltpu.VMEM((r, width), BF16),
            pltpu.VMEM((REMOTE, r, width), BF16),
            pltpu.VMEM((r, width), BF16),
            pltpu.VMEM((r, width), BF16),
            pltpu.VMEM((r, width), F32),
            pltpu.VMEM((REMOTE, r, width), BF16),
            pltpu.VMEM((REMOTE, r, width), BF16),
            pltpu.VMEM((PARTNERS, CHIPS, 2, strip, BLK), F32),
            pltpu.VMEM((PARTNERS, CHIPS, 2, strip, BLK), BF16),
            pltpu.VMEM((PARTNERS, CHIPS, 2, strip, BLK), BF16),
            pltpu.VMEM((PARTNERS, CHIPS, 2, strip, BLK), BF16),
            pltpu.VMEM((CHIPS - 1, PARTNERS, 2, strip, BLK), BF16),
            pltpu.VMEM((2, PARTNERS, strip, BLK), F32),
            dma((3,)),
            dma((3,)),
            dma((REMOTE, CHUNKS)),
            dma((REMOTE, CHUNKS)),
            dma((REMOTE, CHUNKS)),
            dma((REMOTE, CHUNKS)),
            dma((PARTNERS,)),
            dma((PARTNERS,)),
            dma((CHIPS - 1, PARTNERS)),
            dma((CHIPS - 1, PARTNERS)),
        ],
        compiler_params=pltpu.CompilerParams(
            collective_id=0, has_side_effects=True, vmem_limit_bytes=64_000_000
        ),
    )(tokens, weight, cotangent)


def solution(mesh):
    return jax.shard_map(
        local,
        mesh=mesh,
        in_specs=(P("dp", "feat"), P("feat", None, None, None), P("dp", "feat")),
        out_specs=(P("dp", "feat"), P("dp", "feat"), P("feat", None, "dp", None)),
        check_vma=False,
    )
```

time: 470 us -> 201 us (0.43)
  waiting for transfers between devices: 346 us -> 0 us
  Pallas kernels: 0 us -> 191 us
  matrix products: 53.8 us -> 0 us
  local copies, waits for them, and re-layouts: 35.2 us -> 6.59 us
  starting transfers between devices: 19.6 us -> 0 us
  between operations: 14.8 us -> 0.64 us
    unnamed x2 -> x0, waiting for transfers between devices: 195 us -> none
    pallas_call x0 -> x1, Pallas kernels: none -> 191 us  [local(): pl.pallas_call(kernel, out_shape=(jax.ShapeDtypeStruct((r, width), BF16),...]
    ppermute x8 -> x0, waiting for transfers between devices: 151 us -> none  [swapped(): return lax.ppermute(value, axis, pairs)]
    dot_general x18 -> x0, matrix products: 53.8 us -> none  [the longest x6 16.1 us: local(): jnp.einsum('tnb,tnc->nbc', parts[which], delta, preferred_element_type=jn...]
    ppermute x8 -> x0, starting transfers between devices: 19.6 us -> none  [swapped(): return lax.ppermute(value, axis, pairs)]
    another operation x1 -> x0, local copies, waits for them, and re-layouts: 19.2 us -> none  [local(): jnp.stack([jnp.einsum('tnb,tnc->nbc', parts[which], delta, preferred_elem...]
  transfers between devices with their start and end apart: 9 -> 0, of which waited for: 6 -> 0; matrix products, arithmetic and copies ran while one was open for 9% -> 0% of each run, Pallas kernels for 0% -> 0%
where the time goes in v1:
time: 201 us; the launch traced here: 198 us
  Pallas kernels  191 us (95%)
  local copies, waits for them, and re-layouts  6.59 us (3%)
    pallas_call x1, Pallas kernels, local(): pl.pallas_call(kernel, out_shape=(jax.ShapeDtypeStruct((r, width), BF16),...  191 us
    unnamed x3, local copies, waits for them, and re-layouts  6.59 us

profile of v1, /device:TPU:32, one launch (start us, length us, event | category | flops | bytes accessed | tf_op | source)
XLA Modules:
  0.0 198.5 jit_solution(4675116501066179005)
XLA Ops:
  0.6 191.3 %shard_map.58 = (bf16[512,1024]{1,0:T(8,128)(2,1)}, bf16[512,1024]{1,0:T(8,128)(2,1)}, f32[2,6,32,512]{3,2,1,0:T(8,128)}) custom-call(bf16[512,1024]{1,0:T(8,128)(2,1)} %tok_hbm.1, bf16[2,6,512,512]{3,2,1,0:T(8,128)(2,1)} %w_hbm.1, bf16[512,1024]{1,0:T(8,128)(2,1)} %cot_hbm.1), custom_call_target="tpu_custom_call" | custom-call | tf_op jit(solution)/shard_map/pallas_call | solution.py:217
  191.9 2.3 %copy.9 = bf16[512,1024]{1,0:T(8,128)(2,1)} copy(bf16[512,1024]{1,0:T(8,128)(2,1)} %get-tuple-element.6) | data formatting | bytes 2097152
  194.2 2.3 %copy.10 = bf16[512,1024]{1,0:T(8,128)(2,1)} copy(bf16[512,1024]{1,0:T(8,128)(2,1)} %get-tuple-element.7) | data formatting | bytes 2097152
  196.4 2.1 %copy.11 = f32[2,6,32,512]{3,2,1,0:T(8,128)} copy(f32[2,6,32,512]{3,2,1,0:T(8,128)} %get-tuple-element.8) | data formatting | bytes 1572864

commit v2 on v1

--- a/solution.py
+++ b/solution.py
@@ -13,7 +13,8 @@
 BLK = 512
 PARTNERS = 6
 CHUNKS = 8
-REMOTE = 4
+LAG = 4
+FLOWS = 6
 CHIPS = 8
 SLOPE = 0.7978845608028654
 CUBE = 0.044715
@@ -37,7 +38,7 @@
 
 def kernel(
     tok_hbm, w_hbm, cot_hbm, out_hbm, ig_hbm, wg_hbm,
-    tok, w, cot, trecv, delta, outv, acc, tsend, termrecv, mine, other, crecv, total, rsrecv, wgv,
+    tok, w, cot, recv, delta, outv, acc, pool, mine, other, crecv, total, rsrecv, wgv,
     load_sem, store_sem, tok_ssem, tok_rsem, term_ssem, term_rsem, c_ssem, c_rsem, rs_ssem, rs_rsem,
 ):
     rows = tok.shape[0] // CHUNKS
@@ -47,8 +48,16 @@
     chip = d // 2
     y = chip // 2
     x_lo = chip % 2
-
-    partners = [(d, flip(f, 1 << b)) for b in range(REMOTE)]
+    z = f % 8
+    inner = (z + z // 2) % 2
+    sgn = 1 - 2 * ((z // 2) % 2)
+
+    def along(step):
+        return (d, (f // 8) * 8 + (z + step + 8) % 8)
+
+    ahead = along(sgn)
+    behind = along(-sgn)
+    across = (d, flip(f, 8))
     core_mate = (flip(d, 1), f)
 
     def chip_of(j):
@@ -58,7 +67,7 @@
     def mate(j):
         return (chip_of(j) * 2 + core, f)
 
-    everyone = partners + [core_mate]
+    everyone = [ahead, behind, across, core_mate]
     barrier = pltpu.get_barrier_semaphore()
     for who in everyone:
         pl.semaphore_signal(barrier, inc=1, device_id=who, device_id_type=MESH)
@@ -77,53 +86,166 @@
     def span(c):
         return pl.ds(pl.multiple_of(c * rows, rows), rows)
 
-    def tok_copy(b, c):
-        return pltpu.make_async_remote_copy(
-            src_ref=tok.at[span(c)], dst_ref=trecv.at[b, span(c)],
-            send_sem=tok_ssem.at[b, c], recv_sem=tok_rsem.at[b, c],
-            device_id=partners[b], device_id_type=MESH,
-        )
-
-    def term_copy(b, c):
-        return pltpu.make_async_remote_copy(
-            src_ref=tsend.at[b, span(c)], dst_ref=termrecv.at[b, span(c)],
-            send_sem=term_ssem.at[b, c], recv_sem=term_rsem.at[b, c],
-            device_id=partners[b], device_id_type=MESH,
-        )
-
-    @pl.loop(0, CHUNKS)
-    def _(c):
-        for b in (2, 1, 0, 3):
-            tok_copy(b, c).start()
-
-    load_w.wait()
-    load_cot.wait()
-
     def half(n):
         return pl.ds(n * BLK, BLK)
 
-    @pl.loop(0, CHUNKS)
-    def _(c):
+    def tok_copy(flow, c):
+        source, slot, to = (
+            (tok.at[span(c)], 2 * inner, ahead),
+            (recv.at[0, span(c)], 2 * inner + 1, ahead),
+            (recv.at[2, span(c)], 2 * inner, behind),
+            (recv.at[3, span(c)], 2 * inner + 1, behind),
+            (tok.at[span(c)], 4, behind),
+            (tok.at[span(c)], 5, across),
+        )[flow]
+        return pltpu.make_async_remote_copy(
+            src_ref=source, dst_ref=recv.at[slot, span(c)],
+            send_sem=tok_ssem.at[flow, c], recv_sem=tok_rsem.at[slot, c],
+            device_id=to, device_id_type=MESH,
+        )
+
+    def tok_wait(slot, c):
+        pltpu.make_async_remote_copy(
+            src_ref=recv.at[slot, span(c)], dst_ref=recv.at[slot, span(c)],
+            send_sem=tok_ssem.at[0, c], recv_sem=tok_rsem.at[slot, c],
+            device_id=ahead, device_id_type=MESH,
+        ).wait_recv()
+
+    def own(c):
+        @pl.when(c < CHUNKS)
+        def _():
+            tok_copy(0, c).start()
+            tok_copy(5, c).start()
+
+            @pl.when(inner == 1)
+            def _():
+                tok_copy(4, c).start()
+
+    def relay(slot, flow, c):
+        @pl.when((c >= 0) & (c < CHUNKS))
+        def _():
+            tok_wait(slot, c)
+            tok_copy(flow, c).start()
+
+    low = 4 + 2 * (1 - inner)
+
+    def term_copy(flow, c):
+        source, slot, to = (
+            (5 * (1 - inner), low, behind),
+            (2, low + 1, behind),
+            (1 + 5 * inner, low, ahead),
+            (1 + 6 * (1 - inner), low + 1, ahead),
+            (0, 8, ahead),
+            (3, 9, across),
+        )[flow]
+        return pltpu.make_async_remote_copy(
+            src_ref=pool.at[source, span(c)], dst_ref=pool.at[slot, span(c)],
+            send_sem=term_ssem.at[flow, c], recv_sem=term_rsem.at[slot - 4, c],
+            device_id=to, device_id_type=MESH,
+        )
+
+    def term_wait(slot, c):
+        pltpu.make_async_remote_copy(
+            src_ref=pool.at[slot, span(c)], dst_ref=pool.at[slot, span(c)],
+            send_sem=term_ssem.at[0, c], recv_sem=term_rsem.at[slot - 4, c],
+            device_id=ahead, device_id_type=MESH,
+        ).wait_recv()
+
+    def add_term(into, slot, c):
         here = span(c)
-        for b in range(REMOTE):
-            tok_copy(b, c).wait_recv()
+        pool[into, here] = (pool[into, here].astype(F32) + pool[slot, here].astype(F32)).astype(BF16)
+
+    def back_relays(p):
+        c0 = p - 1 - 2 * inner
+
+        @pl.when((c0 >= 0) & (c0 < CHUNKS))
+        def _():
+            term_wait(5, c0)
+
+            @pl.when(inner == 1)
+            def _():
+                add_term(0, 5, c0)
+
+            term_copy(0, c0).start()
+
+        c2 = p - 2 - inner
+
+        @pl.when((c2 >= 0) & (c2 < CHUNKS))
+        def _():
+            term_wait(6, c2)
+
+            @pl.when(inner == 0)
+            def _():
+                add_term(1, 6, c2)
+
+            term_copy(2, c2).start()
+
+        c3 = p - 1 - inner
+
+        @pl.when((c3 >= 0) & (c3 < CHUNKS))
+        def _():
+            term_wait(7, c3)
+
+            @pl.when(inner == 1)
+            def _():
+                add_term(1, 7, c3)
+
+            term_copy(3, c3).start()
+
+    def compute(c):
+        here = span(c)
+        tok_wait(1, c)
+        tok_wait(5, c)
+
+        @pl.when(inner == 0)
+        def _():
+            tok_wait(4, c)
+
+        first = 4 * (1 - inner)
+        second = 2 + inner
         for n in range(2):
-            z = nn(tok[here, half(n)], w[n, 0]) + nn(tok[here, half(1 - n)], w[n, 1])
-            for b in range(REMOTE):
-                z = z + nn(trecv[b, here, half(n)], w[n, b + 2])
-            square = z * z
-            t = jnp.tanh(SLOPE * (z + CUBE * (square * z)))
-            outv[here, half(n)] = (0.5 * z * (1.0 + t)).astype(BF16)
-            slope = 0.5 * (1.0 + t) + 0.5 * z * (1.0 - t * t) * (SLOPE * (1.0 + 3.0 * CUBE * square))
+            v = nn(tok[here, half(n)], w[n, 0]) + nn(tok[here, half(1 - n)], w[n, 1])
+            v = v + nn(recv[first, here, half(n)], w[n, 2]) + nn(recv[second, here, half(n)], w[n, 3])
+            v = v + nn(recv[1, here, half(n)], w[n, 4]) + nn(recv[5, here, half(n)], w[n, 5])
+            square = v * v
+            t = jnp.tanh(SLOPE * (v + CUBE * (square * v)))
+            outv[here, half(n)] = (0.5 * v * (1.0 + t)).astype(BF16)
+            slope = 0.5 * (1.0 + t) + 0.5 * v * (1.0 - t * t) * (SLOPE * (1.0 + 3.0 * CUBE * square))
             delta[here, half(n)] = (cot[here, half(n)].astype(F32) * slope).astype(BF16)
-        for b in (2, 1, 0, 3):
+        for b in (2, 0, 1, 3):
             for n in range(2):
-                tsend[b, here, half(n)] = nt(delta[here, half(n)], w[n, b + 2]).astype(BF16)
-            term_copy(b, c).start()
+                pool[b, here, half(n)] = nt(delta[here, half(n)], w[n, b + 2]).astype(BF16)
+            if b == 2:
+                term_copy(1, c).start()
+            if b == 0:
+                @pl.when(inner == 0)
+                def _():
+                    term_copy(4, c).start()
+            if b == 3:
+                term_copy(5, c).start()
         for n in range(2):
-            own = nt(delta[here, half(n)], w[n, 0]).astype(BF16).astype(F32)
+            mid = nt(delta[here, half(n)], w[n, 0]).astype(BF16).astype(F32)
             side = nt(delta[here, half(1 - n)], w[1 - n, 1]).astype(BF16).astype(F32)
-            acc[here, half(n)] = own + side
+            acc[here, half(n)] = mid + side
+
+    own(0)
+
+    @pl.loop(0, CHUNKS + LAG)
+    def _(i):
+        own(i + 1)
+        relay(0, 1, i - 3 + 2 * inner)
+        relay(2, 2, i - 2 + inner)
+        relay(3, 3, i - 3 + inner)
+
+        @pl.when(i == LAG)
+        def _():
+            load_w.wait()
+            load_cot.wait()
+
+        @pl.when(i >= LAG)
+        def _():
+            compute(i - LAG)
+            back_relays(i - LAG)
 
     store_out = pltpu.make_async_copy(outv, out_hbm, store_sem.at[0])
     store_out.start()
@@ -142,6 +264,8 @@
             device_id=mate(j), device_id_type=MESH,
         )
 
+    first = 4 * (1 - inner)
+    second = 2 + inner
     for k in range(PARTNERS):
         for n in range(2):
             if k == 0:
@@ -149,13 +273,15 @@
             elif k == 1:
                 left = tok[:, half(1 - n)]
             else:
-                left = trecv[k - 2, :, half(n)]
+                left = recv[(first, second, 1, 5)[k - 2], :, half(n)]
             grad = tn(left, delta[:, half(n)])
             grad = grad.reshape(CHIPS, 2, BLK // 16, BLK)
             even, odd = grad[:, 0], grad[:, 1]
             mine[k, :, n] = jnp.where(core == 0, even, odd)
             other[k, :, n] = jnp.where(core == 0, odd, even).astype(BF16)
         core_copy(k).start()
+        if k % 2 == 1:
+            back_relays(CHUNKS + k // 2)
 
     @pl.loop(0, PARTNERS)
     def _(k):
@@ -170,11 +296,15 @@
     @pl.loop(0, CHUNKS)
     def _(c):
         here = span(c)
-        for b in range(REMOTE):
-            term_copy(b, c).wait_recv()
-        result = acc[here, :]
-        for b in range(REMOTE):
-            result = result + termrecv[b, here].astype(F32)
+        term_wait(4, c)
+        term_wait(9, c)
+
+        @pl.when(inner == 1)
+        def _():
+            term_wait(8, c)
+            acc[here, :] += pool[8, here].astype(F32)
+
+        result = acc[here, :] + pool[4, here].astype(F32) + pool[9, here].astype(F32)
         cot[here, :] = result.astype(BF16)
 
     store_ig = pltpu.make_async_copy(cot, ig_hbm, store_sem.at[1])
@@ -195,9 +325,17 @@
 
     @pl.loop(0, CHUNKS)
     def _(c):
-        for b in range(REMOTE):
-            tok_copy(b, c).wait_send()
-            term_copy(b, c).wait_send()
+        for flow in (0, 1, 2, 3, 5):
+            tok_copy(flow, c).wait_send()
+            term_copy(flow, c).wait_send()
+
+        @pl.when(inner == 1)
+        def _():
+            tok_copy(4, c).wait_send()
+
+        @pl.when(inner == 0)
+        def _():
+            term_copy(4, c).wait_send()
 
     @pl.loop(0, PARTNERS)
     def _(k):
@@ -227,12 +365,11 @@
             pltpu.VMEM((r, width), BF16),
             pltpu.VMEM(weight.shape, BF16),
             pltpu.VMEM((r, width), BF16),
-            pltpu.VMEM((REMOTE, r, width), BF16),
+            pltpu.VMEM((FLOWS, r, width), BF16),
             pltpu.VMEM((r, width), BF16),
             pltpu.VMEM((r, width), BF16),
             pltpu.VMEM((r, width), F32),
-            pltpu.VMEM((REMOTE, r, width), BF16),
-            pltpu.VMEM((REMOTE, r, width), BF16),
+            pltpu.VMEM((4 + FLOWS, r, width), BF16),
             pltpu.VMEM((PARTNERS, CHIPS, 2, strip, BLK), F32),
             pltpu.VMEM((PARTNERS, CHIPS, 2, strip, BLK), BF16),
             pltpu.VMEM((PARTNERS, CHIPS, 2, strip, BLK), BF16),
@@ -241,10 +378,10 @@
             pltpu.VMEM((2, PARTNERS, strip, BLK), F32),
             dma((3,)),
             dma((3,)),
-            dma((REMOTE, CHUNKS)),
-            dma((REMOTE, CHUNKS)),
-            dma((REMOTE, CHUNKS)),
-            dma((REMOTE, CHUNKS)),
+            dma((FLOWS, CHUNKS)),
+            dma((FLOWS, CHUNKS)),
+            dma((FLOWS, CHUNKS)),
+            dma((FLOWS, CHUNKS)),
             dma((PARTNERS,)),
             dma((PARTNERS,)),
             dma((CHIPS - 1, PARTNERS)),

time: 201 us -> 175 us (0.87); the launches traced: 198 us -> 175 us
  Pallas kernels: 191 us -> 168 us
    pallas_call x1, Pallas kernels: 191 us -> 168 us  [local(): pl.pallas_call(kernel, out_shape=(jax.ShapeDtypeStruct((r, width), BF16),...]
where the time goes in v2:
time: 175 us
  Pallas kernels  168 us (96%)
  local copies, waits for them, and re-layouts  6.59 us (4%)
    pallas_call x1, Pallas kernels, local(): pl.pallas_call(kernel, out_shape=(jax.ShapeDtypeStruct((r, width), BF16),...  168 us
    unnamed x3, local copies, waits for them, and re-layouts  6.59 us

profile of v2, /device:TPU:32, one launch (start us, length us, event | category | flops | bytes accessed | tf_op | source)
XLA Modules:
  0.0 175.0 jit_solution(3979749594447151186)
XLA Ops:
  0.6 167.8 %shard_map.58 = (bf16[512,1024]{1,0:T(8,128)(2,1)}, bf16[512,1024]{1,0:T(8,128)(2,1)}, f32[2,6,32,512]{3,2,1,0:T(8,128)}) custom-call(bf16[512,1024]{1,0:T(8,128)(2,1)} %tok_hbm.1, bf16[2,6,512,512]{3,2,1,0:T(8,128)(2,1)} %w_hbm.1, bf16[512,1024]{1,0:T(8,128)(2,1)} %cot_hbm.1), custom_call_target="tpu_custom_call" | custom-call | tf_op jit(solution)/shard_map/pallas_call | solution.py:355
  168.4 2.3 %copy.9 = bf16[512,1024]{1,0:T(8,128)(2,1)} copy(bf16[512,1024]{1,0:T(8,128)(2,1)} %get-tuple-element.6) | data formatting | bytes 2097152
  170.7 2.3 %copy.10 = bf16[512,1024]{1,0:T(8,128)(2,1)} copy(bf16[512,1024]{1,0:T(8,128)(2,1)} %get-tuple-element.7) | data formatting | bytes 2097152
  173.0 2.1 %copy.11 = f32[2,6,32,512]{3,2,1,0:T(8,128)} copy(f32[2,6,32,512]{3,2,1,0:T(8,128)} %get-tuple-element.8) | data formatting | bytes 1572864

commit v3 on v2

--- a/solution.py
+++ b/solution.py
@@ -14,6 +14,7 @@
 PARTNERS = 6
 CHUNKS = 8
 LAG = 4
+BACK = 3
 FLOWS = 6
 CHIPS = 8
 SLOPE = 0.7978845608028654
@@ -155,7 +156,11 @@
         here = span(c)
         pool[into, here] = (pool[into, here].astype(F32) + pool[slot, here].astype(F32)).astype(BF16)
 
-    def back_relays(p):
+    def back_step(p):
+        @pl.when((p >= 0) & (p < CHUNKS))
+        def _():
+            term_copy(1, p).start()
+
         c0 = p - 1 - 2 * inner
 
         @pl.when((c0 >= 0) & (c0 < CHUNKS))
@@ -212,11 +217,9 @@
             outv[here, half(n)] = (0.5 * v * (1.0 + t)).astype(BF16)
             slope = 0.5 * (1.0 + t) + 0.5 * v * (1.0 - t * t) * (SLOPE * (1.0 + 3.0 * CUBE * square))
             delta[here, half(n)] = (cot[here, half(n)].astype(F32) * slope).astype(BF16)
-        for b in (2, 0, 1, 3):
+        for b in (0, 3, 2, 1):
             for n in range(2):
                 pool[b, here, half(n)] = nt(delta[here, half(n)], w[n, b + 2]).astype(BF16)
-            if b == 2:
-                term_copy(1, c).start()
             if b == 0:
                 @pl.when(inner == 0)
                 def _():
@@ -245,7 +248,7 @@
         @pl.when(i >= LAG)
         def _():
             compute(i - LAG)
-            back_relays(i - LAG)
+            back_step(i - LAG - BACK)
 
     store_out = pltpu.make_async_copy(outv, out_hbm, store_sem.at[0])
     store_out.start()
@@ -266,7 +269,8 @@
 
     first = 4 * (1 - inner)
     second = 2 + inner
-    for k in range(PARTNERS):
+
+    def weight_grad(k):
         for n in range(2):
             if k == 0:
                 left = tok[:, half(n)]
@@ -280,11 +284,8 @@
             mine[k, :, n] = jnp.where(core == 0, even, odd)
             other[k, :, n] = jnp.where(core == 0, odd, even).astype(BF16)
         core_copy(k).start()
-        if k % 2 == 1:
-            back_relays(CHUNKS + k // 2)
-
-    @pl.loop(0, PARTNERS)
-    def _(k):
+
+    def pair_sum(k):
         core_copy(k).wait_recv()
         for q in range(CHIPS):
             both = mine[k, q] + crecv[k, q].astype(F32)
@@ -292,6 +293,17 @@
             total[k, q] = both.astype(BF16)
         for j in range(1, CHIPS):
             rs_copy(k, j).start()
+
+    todo = [(weight_grad, 0), (weight_grad, 1), (weight_grad, 2)]
+    for k in range(PARTNERS):
+        todo.append((pair_sum, k))
+        if k + 3 < PARTNERS:
+            todo.append((weight_grad, k + 3))
+    steps = BACK + 3
+    for t in range(steps):
+        back_step(CHUNKS - BACK + t)
+        for work, k in todo[t * len(todo) // steps : (t + 1) * len(todo) // steps]:
+            work(k)
 
     @pl.loop(0, CHUNKS)
     def _(c):

time: 175 us -> 166 us (0.949)
  Pallas kernels: 168 us -> 158 us
    pallas_call x1, Pallas kernels: 168 us -> 158 us  [local(): pl.pallas_call(kernel, out_shape=(jax.ShapeDtypeStruct((r, width), BF16),...]
where the time goes in v3:
time: 166 us; the launch traced here: 165 us
  Pallas kernels  158 us (95%)
  local copies, waits for them, and re-layouts  6.59 us (4%)
    pallas_call x1, Pallas kernels, local(): pl.pallas_call(kernel, out_shape=(jax.ShapeDtypeStruct((r, width), BF16),...  158 us
    unnamed x3, local copies, waits for them, and re-layouts  6.59 us

profile of v3, /device:TPU:32, one launch (start us, length us, event | category | flops | bytes accessed | tf_op | source)
XLA Modules:
  0.0 165.4 jit_solution(14695732143203208408)
XLA Ops:
  0.6 158.2 %shard_map.58 = (bf16[512,1024]{1,0:T(8,128)(2,1)}, bf16[512,1024]{1,0:T(8,128)(2,1)}, f32[2,6,32,512]{3,2,1,0:T(8,128)}) custom-call(bf16[512,1024]{1,0:T(8,128)(2,1)} %tok_hbm.1, bf16[2,6,512,512]{3,2,1,0:T(8,128)(2,1)} %w_hbm.1, bf16[512,1024]{1,0:T(8,128)(2,1)} %cot_hbm.1), custom_call_target="tpu_custom_call" | custom-call | tf_op jit(solution)/shard_map/pallas_call | solution.py:367
  158.8 2.3 %copy.9 = bf16[512,1024]{1,0:T(8,128)(2,1)} copy(bf16[512,1024]{1,0:T(8,128)(2,1)} %get-tuple-element.6) | data formatting | bytes 2097152
  161.1 2.3 %copy.10 = bf16[512,1024]{1,0:T(8,128)(2,1)} copy(bf16[512,1024]{1,0:T(8,128)(2,1)} %get-tuple-element.7) | data formatting | bytes 2097152
  163.3 2.1 %copy.11 = f32[2,6,32,512]{3,2,1,0:T(8,128)} copy(f32[2,6,32,512]{3,2,1,0:T(8,128)} %get-tuple-element.8) | data formatting | bytes 1572864

commit v4 on v3

--- a/solution.py
+++ b/solution.py
@@ -12,9 +12,11 @@
 MESH = pl.DeviceIdType.MESH
 BLK = 512
 PARTNERS = 6
-CHUNKS = 8
-LAG = 4
-BACK = 3
+CHUNKS = 16
+HOP = 2
+LAG = 8
+SPREAD = 5
+BACK = 8
 FLOWS = 6
 CHIPS = 8
 SLOPE = 0.7978845608028654
@@ -87,6 +89,9 @@
     def span(c):
         return pl.ds(pl.multiple_of(c * rows, rows), rows)
 
+    def pair_span(q):
+        return pl.ds(pl.multiple_of(q * 2 * rows, 2 * rows), 2 * rows)
+
     def half(n):
         return pl.ds(n * BLK, BLK)
 
@@ -161,7 +166,7 @@
         def _():
             term_copy(1, p).start()
 
-        c0 = p - 1 - 2 * inner
+        c0 = p - HOP * (1 + 2 * inner)
 
         @pl.when((c0 >= 0) & (c0 < CHUNKS))
         def _():
@@ -173,7 +178,7 @@
 
             term_copy(0, c0).start()
 
-        c2 = p - 2 - inner
+        c2 = p - HOP * (2 + inner)
 
         @pl.when((c2 >= 0) & (c2 < CHUNKS))
         def _():
@@ -185,7 +190,7 @@
 
             term_copy(2, c2).start()
 
-        c3 = p - 1 - inner
+        c3 = p - HOP * (1 + inner)
 
         @pl.when((c3 >= 0) & (c3 < CHUNKS))
         def _():
@@ -197,14 +202,16 @@
 
             term_copy(3, c3).start()
 
-    def compute(c):
-        here = span(c)
-        tok_wait(1, c)
-        tok_wait(5, c)
+    def forward(q):
+        here = pair_span(q)
+        for c in (2 * q, 2 * q + 1):
+            tok_wait(1, c)
+            tok_wait(5, c)
 
         @pl.when(inner == 0)
         def _():
-            tok_wait(4, c)
+            tok_wait(4, 2 * q)
+            tok_wait(4, 2 * q + 1)
 
         first = 4 * (1 - inner)
         second = 2 + inner
@@ -217,15 +224,20 @@
             outv[here, half(n)] = (0.5 * v * (1.0 + t)).astype(BF16)
             slope = 0.5 * (1.0 + t) + 0.5 * v * (1.0 - t * t) * (SLOPE * (1.0 + 3.0 * CUBE * square))
             delta[here, half(n)] = (cot[here, half(n)].astype(F32) * slope).astype(BF16)
+
+    def backward(q):
+        here = pair_span(q)
         for b in (0, 3, 2, 1):
             for n in range(2):
                 pool[b, here, half(n)] = nt(delta[here, half(n)], w[n, b + 2]).astype(BF16)
             if b == 0:
                 @pl.when(inner == 0)
                 def _():
-                    term_copy(4, c).start()
+                    term_copy(4, 2 * q).start()
+                    term_copy(4, 2 * q + 1).start()
             if b == 3:
-                term_copy(5, c).start()
+                term_copy(5, 2 * q).start()
+                term_copy(5, 2 * q + 1).start()
         for n in range(2):
             mid = nt(delta[here, half(n)], w[n, 0]).astype(BF16).astype(F32)
             side = nt(delta[here, half(1 - n)], w[1 - n, 1]).astype(BF16).astype(F32)
@@ -236,19 +248,25 @@
     @pl.loop(0, CHUNKS + LAG)
     def _(i):
         own(i + 1)
-        relay(0, 1, i - 3 + 2 * inner)
-        relay(2, 2, i - 2 + inner)
-        relay(3, 3, i - 3 + inner)
-
-        @pl.when(i == LAG)
+        relay(0, 1, i - HOP * (3 - 2 * inner))
+        relay(2, 2, i - HOP * (2 - inner))
+        relay(3, 3, i - HOP * (3 - inner))
+        q = i - LAG
+
+        @pl.when(q == 0)
         def _():
             load_w.wait()
             load_cot.wait()
 
-        @pl.when(i >= LAG)
-        def _():
-            compute(i - LAG)
-            back_step(i - LAG - BACK)
+        @pl.when((q >= 0) & (q % 2 == 0))
+        def _():
+            forward(q // 2)
+
+        @pl.when((q >= 0) & (q % 2 == 1))
+        def _():
+            backward(q // 2)
+
+        back_step(q - 1 - BACK)
 
     store_out = pltpu.make_async_copy(outv, out_hbm, store_sem.at[0])
     store_out.start()
@@ -299,10 +317,9 @@
         todo.append((pair_sum, k))
         if k + 3 < PARTNERS:
             todo.append((weight_grad, k + 3))
-    steps = BACK + 3
-    for t in range(steps):
-        back_step(CHUNKS - BACK + t)
-        for work, k in todo[t * len(todo) // steps : (t + 1) * len(todo) // steps]:
+    for t in range(BACK + 1 + 3 * HOP):
+        back_step(CHUNKS - 1 - BACK + t)
+        for work, k in todo[t * len(todo) // SPREAD : (t + 1) * len(todo) // SPREAD]:
             work(k)
 
     @pl.loop(0, CHUNKS)

time: 166 us -> 154 us (0.928)
  Pallas kernels: 158 us -> 146 us
    pallas_call x1, Pallas kernels: 158 us -> 146 us  [local(): pl.pallas_call(kernel, out_shape=(jax.ShapeDtypeStruct((r, width), BF16),...]
where the time goes in v4:
time: 154 us; the launch traced here: 153 us
  Pallas kernels  146 us (95%)
  local copies, waits for them, and re-layouts  6.59 us (4%)
    pallas_call x1, Pallas kernels, local(): pl.pallas_call(kernel, out_shape=(jax.ShapeDtypeStruct((r, width), BF16),...  146 us
    unnamed x3, local copies, waits for them, and re-layouts  6.59 us

profile of v4, /device:TPU:32, one launch (start us, length us, event | category | flops | bytes accessed | tf_op | source)
XLA Modules:
  0.0 153.2 jit_solution(15238333735215526263)
XLA Ops:
  0.6 146.0 %shard_map.58 = (bf16[512,1024]{1,0:T(8,128)(2,1)}, bf16[512,1024]{1,0:T(8,128)(2,1)}, f32[2,6,32,512]{3,2,1,0:T(8,128)}) custom-call(bf16[512,1024]{1,0:T(8,128)(2,1)} %tok_hbm.1, bf16[2,6,512,512]{3,2,1,0:T(8,128)(2,1)} %w_hbm.1, bf16[512,1024]{1,0:T(8,128)(2,1)} %cot_hbm.1), custom_call_target="tpu_custom_call" | custom-call | tf_op jit(solution)/shard_map/pallas_call | solution.py:384
  146.7 2.3 %copy.9 = bf16[512,1024]{1,0:T(8,128)(2,1)} copy(bf16[512,1024]{1,0:T(8,128)(2,1)} %get-tuple-element.6) | data formatting | bytes 2097152
  148.9 2.3 %copy.10 = bf16[512,1024]{1,0:T(8,128)(2,1)} copy(bf16[512,1024]{1,0:T(8,128)(2,1)} %get-tuple-element.7) | data formatting | bytes 2097152
  151.2 2.1 %copy.11 = f32[2,6,32,512]{3,2,1,0:T(8,128)} copy(f32[2,6,32,512]{3,2,1,0:T(8,128)} %get-tuple-element.8) | data formatting | bytes 1572864

commit v5 on v4

--- a/solution.py
+++ b/solution.py
@@ -15,8 +15,10 @@
 CHUNKS = 16
 HOP = 2
 LAG = 8
+LAST = 4
 SPREAD = 5
-BACK = 8
+EARLY = 6
+BACK = 10
 FLOWS = 6
 CHIPS = 8
 SLOPE = 0.7978845608028654
@@ -162,11 +164,13 @@
         pool[into, here] = (pool[into, here].astype(F32) + pool[slot, here].astype(F32)).astype(BF16)
 
     def back_step(p):
-        @pl.when((p >= 0) & (p < CHUNKS))
-        def _():
-            term_copy(1, p).start()
-
-        c0 = p - HOP * (1 + 2 * inner)
+        c1 = p + EARLY * (1 - inner)
+
+        @pl.when((c1 >= 0) & (c1 < CHUNKS))
+        def _():
+            term_copy(1, c1).start()
+
+        c0 = p - HOP * (1 + 2 * inner) + EARLY * inner
 
         @pl.when((c0 >= 0) & (c0 < CHUNKS))
         def _():
@@ -190,7 +194,7 @@
 
             term_copy(2, c2).start()
 
-        c3 = p - HOP * (1 + inner)
+        c3 = p - HOP * (1 + inner) + EARLY
 
         @pl.when((c3 >= 0) & (c3 < CHUNKS))
         def _():
@@ -306,9 +310,7 @@
     def pair_sum(k):
         core_copy(k).wait_recv()
         for q in range(CHIPS):
-            both = mine[k, q] + crecv[k, q].astype(F32)
-            mine[k, q] = both
-            total[k, q] = both.astype(BF16)
+            total[k, q] = (mine[k, q] + crecv[k, q].astype(F32)).astype(BF16)
         for j in range(1, CHIPS):
             rs_copy(k, j).start()
 
@@ -322,8 +324,7 @@
         for work, k in todo[t * len(todo) // SPREAD : (t + 1) * len(todo) // SPREAD]:
             work(k)
 
-    @pl.loop(0, CHUNKS)
-    def _(c):
+    def gather_terms(c):
         here = span(c)
         term_wait(4, c)
         term_wait(9, c)
@@ -336,14 +337,18 @@
         result = acc[here, :] + pool[4, here].astype(F32) + pool[9, here].astype(F32)
         cot[here, :] = result.astype(BF16)
 
-    store_ig = pltpu.make_async_copy(cot, ig_hbm, store_sem.at[1])
-    store_ig.start()
+    def store_ig(c, size):
+        part = pl.ds(c * rows, size * rows)
+        return pltpu.make_async_copy(cot.at[part], ig_hbm.at[part], store_sem.at[1 if c == 0 else 3])
+
+    pl.loop(0, CHUNKS - LAST)(gather_terms)
+    store_ig(0, CHUNKS - LAST).start()
 
     @pl.loop(0, PARTNERS)
     def _(k):
         for j in range(1, CHIPS):
             rs_copy(k, j).wait_recv()
-        summed = mine[k, chip]
+        summed = mine[k, chip] + crecv[k, chip].astype(F32)
         for j in range(1, CHIPS):
             summed = summed + rsrecv[j - 1, k].astype(F32)
         for n in range(2):
@@ -351,6 +356,8 @@
 
     store_wg = pltpu.make_async_copy(wgv, wg_hbm, store_sem.at[2])
     store_wg.start()
+    pl.loop(CHUNKS - LAST, CHUNKS)(gather_terms)
+    store_ig(CHUNKS - LAST, LAST).start()
 
     @pl.loop(0, CHUNKS)
     def _(c):
@@ -373,15 +380,29 @@
             rs_copy(k, j).wait_send()
 
     store_out.wait()
-    store_ig.wait()
+    store_ig(0, CHUNKS - LAST).wait()
+    store_ig(CHUNKS - LAST, LAST).wait()
     store_wg.wait()
+
+
+def place(*refs):
+    arrays, outs, buffers, sems = refs[:3], refs[3:6], refs[6:9], refs[9]
+    reads = [pltpu.make_async_copy(a, b, sems.at[0, i]) for i, (a, b) in enumerate(zip(arrays, buffers))]
+    writes = [pltpu.make_async_copy(b, o, sems.at[1, i]) for i, (b, o) in enumerate(zip(buffers, outs))]
+    for read in reads:
+        read.start()
+    for read, write in zip(reads, writes):
+        read.wait()
+        write.start()
+    for write in writes:
+        write.wait()
 
 
 def local(tokens, weight, cotangent):
     r, width = tokens.shape
     strip = BLK // 16
     dma = pltpu.SemaphoreType.DMA
-    return pl.pallas_call(
+    results = pl.pallas_call(
         kernel,
         out_shape=(
             jax.ShapeDtypeStruct((r, width), BF16),
@@ -406,7 +427,7 @@
             pltpu.VMEM((CHIPS - 1, PARTNERS, 2, strip, BLK), BF16),
             pltpu.VMEM((2, PARTNERS, strip, BLK), F32),
             dma((3,)),
-            dma((3,)),
+            dma((4,)),
             dma((FLOWS, CHUNKS)),
             dma((FLOWS, CHUNKS)),
             dma((FLOWS, CHUNKS)),
@@ -420,6 +441,13 @@
             collective_id=0, has_side_effects=True, vmem_limit_bytes=64_000_000
         ),
     )(tokens, weight, cotangent)
+    return pl.pallas_call(
+        place,
+        out_shape=tuple(jax.ShapeDtypeStruct(a.shape, a.dtype) for a in results),
+        in_specs=[pl.BlockSpec(memory_space=pl.ANY)] * 3,
+        out_specs=[pl.BlockSpec(memory_space=pl.ANY)] * 3,
+        scratch_shapes=[pltpu.VMEM(a.shape, a.dtype) for a in results] + [dma((2, 3))],
+    )(*results)
 
 
 def solution(mesh):

time: 154 us -> 147 us (0.955)
  local copies, waits for them, and re-layouts: 6.59 us -> 0 us
    unnamed x3 -> x0, local copies, waits for them, and re-layouts: 6.59 us -> none
    pallas_call x0 -> x1, Pallas kernels: none -> 2.85 us  [local(): pl.pallas_call(place, out_shape=tuple((jax.ShapeDtypeStruct(a.shape, a.dt...]
    pallas_call x1, Pallas kernels: 146 us -> 144 us  [local(): pl.pallas_call(kernel, out_shape=(jax.ShapeDtypeStruct((r, width), BF16),...]
where the time goes in v5:
time: 147 us
  Pallas kernels  146 us (99%)
    pallas_call x1, Pallas kernels, local(): pl.pallas_call(kernel, out_shape=(jax.ShapeDtypeStruct((r, width), BF16),...  144 us

profile of v5, /device:TPU:32, one launch (start us, length us, event | category | flops | bytes accessed | tf_op | source)
XLA Modules:
  0.0 147.1 jit_solution(16384235864446135918)
XLA Ops:
  0.6 143.6 %shard_map.58 = (bf16[512,1024]{1,0:T(8,128)(2,1)}, bf16[512,1024]{1,0:T(8,128)(2,1)}, f32[2,6,32,512]{3,2,1,0:T(8,128)}) custom-call(bf16[512,1024]{1,0:T(8,128)(2,1)} %tok_hbm.1, bf16[2,6,512,512]{3,2,1,0:T(8,128)(2,1)} %w_hbm.1, bf16[512,1024]{1,0:T(8,128)(2,1)} %cot_hbm.1), custom_call_target="tpu_custom_call" | custom-call | tf_op jit(solution)/shard_map/pallas_call | solution.py:405
  144.2 2.8 %shard_map.59 = (bf16[512,1024]{1,0:T(8,128)(2,1)}, bf16[512,1024]{1,0:T(8,128)(2,1)}, f32[2,6,32,512]{3,2,1,0:T(8,128)}) custom-call(bf16[512,1024]{1,0:T(8,128)(2,1)} %get-tuple-element.6.refs_0_, bf16[512,1024]{1,0:T(8,128)(2,1)} %get-tuple-element.7.refs_1_, f32[2,6,32,512]{3,2,1,0:T(8,128)} %get-tuple-element.8.refs_2_), custom_call_target="tpu_custom_call" | custom-call | tf_op jit(solution)/shard_map/pallas_call | solution.py:444

commit v6 on v5

--- a/solution.py
+++ b/solution.py
@@ -42,9 +42,9 @@
 
 
 def kernel(
-    tok_hbm, w_hbm, cot_hbm, out_hbm, ig_hbm, wg_hbm,
-    tok, w, cot, recv, delta, outv, acc, pool, mine, other, crecv, total, rsrecv, wgv,
-    load_sem, store_sem, tok_ssem, tok_rsem, term_ssem, term_rsem, c_ssem, c_rsem, rs_ssem, rs_rsem,
+    tok_hbm, w_hbm, cot_hbm, outv, ig, wgv,
+    tok, w, cot, recv, delta, acc, pool, mine, other, crecv, total, rsrecv,
+    load_sem, tok_ssem, tok_rsem, term_ssem, term_rsem, c_ssem, c_rsem, rs_ssem, rs_rsem,
 ):
     rows = tok.shape[0] // CHUNKS
     d = lax.axis_index("dp")
@@ -272,9 +272,6 @@
 
         back_step(q - 1 - BACK)
 
-    store_out = pltpu.make_async_copy(outv, out_hbm, store_sem.at[0])
-    store_out.start()
-
     def core_copy(k):
         return pltpu.make_async_remote_copy(
             src_ref=other.at[k], dst_ref=crecv.at[k],
@@ -335,14 +332,9 @@
             acc[here, :] += pool[8, here].astype(F32)
 
         result = acc[here, :] + pool[4, here].astype(F32) + pool[9, here].astype(F32)
-        cot[here, :] = result.astype(BF16)
-
-    def store_ig(c, size):
-        part = pl.ds(c * rows, size * rows)
-        return pltpu.make_async_copy(cot.at[part], ig_hbm.at[part], store_sem.at[1 if c == 0 else 3])
+        ig[here, :] = result.astype(BF16)
 
     pl.loop(0, CHUNKS - LAST)(gather_terms)
-    store_ig(0, CHUNKS - LAST).start()
 
     @pl.loop(0, PARTNERS)
     def _(k):
@@ -354,10 +346,7 @@
         for n in range(2):
             wgv[n, k] = summed[n]
 
-    store_wg = pltpu.make_async_copy(wgv, wg_hbm, store_sem.at[2])
-    store_wg.start()
     pl.loop(CHUNKS - LAST, CHUNKS)(gather_terms)
-    store_ig(CHUNKS - LAST, LAST).start()
 
     @pl.loop(0, CHUNKS)
     def _(c):
@@ -379,20 +368,11 @@
         for j in range(1, CHIPS):
             rs_copy(k, j).wait_send()
 
-    store_out.wait()
-    store_ig(0, CHUNKS - LAST).wait()
-    store_ig(CHUNKS - LAST, LAST).wait()
-    store_wg.wait()
-
 
 def place(*refs):
-    arrays, outs, buffers, sems = refs[:3], refs[3:6], refs[6:9], refs[9]
-    reads = [pltpu.make_async_copy(a, b, sems.at[0, i]) for i, (a, b) in enumerate(zip(arrays, buffers))]
-    writes = [pltpu.make_async_copy(b, o, sems.at[1, i]) for i, (b, o) in enumerate(zip(buffers, outs))]
-    for read in reads:
-        read.start()
-    for read, write in zip(reads, writes):
-        read.wait()
+    arrays, outs, sem = refs[:3], refs[3:6], refs[6]
+    writes = [pltpu.make_async_copy(a, o, sem.at[i]) for i, (a, o) in enumerate(zip(arrays, outs))]
+    for write in writes:
         write.start()
     for write in writes:
         write.wait()
@@ -405,18 +385,17 @@
     results = pl.pallas_call(
         kernel,
         out_shape=(
-            jax.ShapeDtypeStruct((r, width), BF16),
-            jax.ShapeDtypeStruct((r, width), BF16),
-            jax.ShapeDtypeStruct((2, PARTNERS, strip, BLK), F32),
+            pltpu.VMEM((r, width), BF16),
+            pltpu.VMEM((r, width), BF16),
+            pltpu.VMEM((2, PARTNERS, strip, BLK), F32),
         ),
-        in_specs=[pl.BlockSpec(memory_space=pl.ANY)] * 3,
-        out_specs=[pl.BlockSpec(memory_space=pl.ANY)] * 3,
+        in_specs=[pl.BlockSpec(memory_space=pltpu.HBM)] * 3,
+        out_specs=[pl.BlockSpec(memory_space=pltpu.VMEM)] * 3,
         scratch_shapes=[
             pltpu.VMEM((r, width), BF16),
             pltpu.VMEM(weight.shape, BF16),
             pltpu.VMEM((r, width), BF16),
             pltpu.VMEM((FLOWS, r, width), BF16),
-            pltpu.VMEM((r, width), BF16),
             pltpu.VMEM((r, width), BF16),
             pltpu.VMEM((r, width), F32),
             pltpu.VMEM((4 + FLOWS, r, width), BF16),
@@ -425,9 +404,7 @@
             pltpu.VMEM((PARTNERS, CHIPS, 2, strip, BLK), BF16),
             pltpu.VMEM((PARTNERS, CHIPS, 2, strip, BLK), BF16),
             pltpu.VMEM((CHIPS - 1, PARTNERS, 2, strip, BLK), BF16),
-            pltpu.VMEM((2, PARTNERS, strip, BLK), F32),
             dma((3,)),
-            dma((4,)),
             dma((FLOWS, CHUNKS)),
             dma((FLOWS, CHUNKS)),
             dma((FLOWS, CHUNKS)),
@@ -438,7 +415,7 @@
             dma((CHIPS - 1, PARTNERS)),
         ],
         compiler_params=pltpu.CompilerParams(
-            collective_id=0, has_side_effects=True, vmem_limit_bytes=64_000_000
+            collective_id=0, has_side_effects=True, vmem_limit_bytes=63_500_000
         ),
     )(tokens, weight, cotangent)
     return pl.pallas_call(
@@ -446,7 +423,8 @@
         out_shape=tuple(jax.ShapeDtypeStruct(a.shape, a.dtype) for a in results),
         in_specs=[pl.BlockSpec(memory_space=pl.ANY)] * 3,
         out_specs=[pl.BlockSpec(memory_space=pl.ANY)] * 3,
-        scratch_shapes=[pltpu.VMEM(a.shape, a.dtype) for a in results] + [dma((2, 3))],
+        scratch_shapes=[dma((3,))],
+        compiler_params=pltpu.CompilerParams(vmem_limit_bytes=4_000_000),
     )(*results)
 
 

time: 147 us -> 146 us (level)
  no operation moved by 1% of the time
where the time goes in v6:
time: 146 us; the launch traced here: 145 us
  Pallas kernels  145 us (99%)
    pallas_call x1, Pallas kernels, local(): pl.pallas_call(kernel, out_shape=(pltpu.VMEM((r, width), BF16), pltpu.VME...  143 us

profile of v6, /device:TPU:32, one launch (start us, length us, event | category | flops | bytes accessed | tf_op | source)
XLA Modules:
  0.0 145.5 jit_solution(8406401622908816309)
XLA Ops:
  0.6 143.2 %shard_map.58 = (bf16[512,1024]{1,0:T(8,128)(2,1)S(1)}, bf16[512,1024]{1,0:T(8,128)(2,1)S(1)}, f32[2,6,32,512]{3,2,1,0:T(8,128)S(1)}) custom-call(bf16[512,1024]{1,0:T(8,128)(2,1)} %tok_hbm.1, bf16[2,6,512,512]{3,2,1,0:T(8,128)(2,1)} %w_hbm.1, bf16[512,1024]{1,0:T(8,128)(2,1)} %cot_hbm.1), custom_call_target="tpu_custom_call" | custom-call | tf_op jit(solution)/shard_map/pallas_call | solution.py:385
  143.9 1.6 %shard_map.59 = (bf16[512,1024]{1,0:T(8,128)(2,1)}, bf16[512,1024]{1,0:T(8,128)(2,1)}, f32[2,6,32,512]{3,2,1,0:T(8,128)}) custom-call(bf16[512,1024]{1,0:T(8,128)(2,1)S(1)} %get-tuple-element.6.refs_0_, bf16[512,1024]{1,0:T(8,128)(2,1)S(1)} %get-tuple-element.7.refs_1_, f32[2,6,32,512]{3,2,1,0:T(8,128)S(1)} %get-tuple-element.8.refs_2_), custom_call_target="tpu_custom_call" | custom-call | tf_op jit(solution)/shard_map/pallas_call | solution.py:421

commit v7 on v6

--- a/solution.py
+++ b/solution.py
@@ -14,11 +14,11 @@
 PARTNERS = 6
 CHUNKS = 16
 HOP = 2
-LAG = 8
+LAG = 9
 LAST = 4
 SPREAD = 5
 EARLY = 6
-BACK = 10
+BACK = 9
 FLOWS = 6
 CHIPS = 8
 SLOPE = 0.7978845608028654

time: 146 us -> 147 us (level)
  Pallas kernels: 145 us -> 147 us
    pallas_call x1, Pallas kernels: 143 us -> 145 us  [local(): pl.pallas_call(kernel, out_shape=(pltpu.VMEM((r, width), BF16), pltpu.VME...]
where the time goes in v7:
time: 147 us
  Pallas kernels  147 us (100%)
    pallas_call x1, Pallas kernels, local(): pl.pallas_call(kernel, out_shape=(pltpu.VMEM((r, width), BF16), pltpu.VME...  145 us

profile of v7, /device:TPU:32, one launch (start us, length us, event | category | flops | bytes accessed | tf_op | source)
XLA Modules:
  0.0 147.2 jit_solution(8967021146172122494)
XLA Ops:
  0.6 144.9 %shard_map.58 = (bf16[512,1024]{1,0:T(8,128)(2,1)S(1)}, bf16[512,1024]{1,0:T(8,128)(2,1)S(1)}, f32[2,6,32,512]{3,2,1,0:T(8,128)S(1)}) custom-call(bf16[512,1024]{1,0:T(8,128)(2,1)} %tok_hbm.1, bf16[2,6,512,512]{3,2,1,0:T(8,128)(2,1)} %w_hbm.1, bf16[512,1024]{1,0:T(8,128)(2,1)} %cot_hbm.1), custom_call_target="tpu_custom_call" | custom-call | tf_op jit(solution)/shard_map/pallas_call | solution.py:385
  145.6 1.6 %shard_map.59 = (bf16[512,1024]{1,0:T(8,128)(2,1)}, bf16[512,1024]{1,0:T(8,128)(2,1)}, f32[2,6,32,512]{3,2,1,0:T(8,128)}) custom-call(bf16[512,1024]{1,0:T(8,128)(2,1)S(1)} %get-tuple-element.6.refs_0_, bf16[512,1024]{1,0:T(8,128)(2,1)S(1)} %get-tuple-element.7.refs_1_, f32[2,6,32,512]{3,2,1,0:T(8,128)S(1)} %get-tuple-element.8.refs_2_), custom_call_target="tpu_custom_call" | custom-call | tf_op jit(solution)/shard_map/pallas_call | solution.py:421
